TPU v7x, 256 devices: a whole 4x4x8 slice. The times are simulated.
256 devices in a mesh: seq: 32 (over z, x), fsdp: 8 (over y, core).
Axes of the slice: x: 4, y: 4, z: 8, core: 2. Of those that a mesh axis runs over, the one named last changes fastest.
Arguments:
- tokens: bfloat16 [24576, 6144], P('seq'), may hold values from -30 to 30
- w_query: bfloat16 [6144, 32, 128], P('seq', 'fsdp'), may hold values from -0.078125 to 0.078125
- w_keyval: bfloat16 [6144, 32, 256], P('seq', 'fsdp'), may hold values from -40 to 40
- doc_lengths: int32 [8], replicated, may hold values from 1 to 12288, 24576 in all
- norm_gain: bfloat16 [4096], P('fsdp'), may hold values from 0.25 to 1.75
Outputs:
- attended: bfloat16 [24576, 4096], P('seq', 'fsdp')
Inputs may be any that keep to these rules, and one draw needn't show every extreme that they name: `doc_lengths`: lengths are positive and sum to 24576; the longest document has exactly 12288 tokens.
All inputs are finite; a program needn't handle non-finite values.
Results may differ from a plain program's by a relative error of at most 0.0034.
Values may be sent and summed in bfloat16 or wider, within the bound.
A program may use at most 128 MiB of HBM per device.

v0:
```python
import jax
import jax.numpy as jnp
from jax import lax
from jax.sharding import PartitionSpec as P


def carried_in(value, axis, join, neutral):
    count, mine = (lax.axis_size(axis), lax.axis_index(axis))
    pieces = jax.tree.map(lambda part: lax.all_gather(part, axis), value)
    running = jax.tree.map(
        lambda part, zero: jnp.full_like(part, 0) + jnp.asarray(zero, part.dtype), value, neutral
    )

    def step(position, running):
        longer = join(running, jax.tree.map(lambda part: part[position], pieces))
        return jax.tree.map(lambda new, old: jnp.where(position < mine, new, old), longer, running)

    return lax.fori_loop(0, count - 1, step, running)


def doc_index(positions, doc_ends):
    return jnp.sum((positions[:, None] >= doc_ends[None, :]).astype(jnp.int32), axis=1)


def shards(tokens, w_query, w_keyval, doc_lengths, norm_gain):
    rows_here = tokens.shape[0]
    head_count = w_query.shape[1]
    head_size = w_query.shape[2]
    shard_index = lax.axis_index("seq")
    doc_ends = jnp.cumsum(doc_lengths)
    offsets = lax.iota(jnp.int32, rows_here)
    doc_ids = doc_index(shard_index * rows_here + offsets, doc_ends)
    first_doc = doc_ids[0]
    tail_doc = doc_ids[rows_here - 1]

    def project(panel_rows):
        panel = panel_rows.reshape(panel_rows.shape[0], panel_rows.shape[1] * panel_rows.shape[2])
        return jnp.dot(tokens, panel, preferred_element_type=jnp.float32)

    query_sum = project(lax.all_gather(w_query, "seq", axis=0, tiled=True))
    keyval_sum = project(lax.all_gather(w_keyval, "seq", axis=0, tiled=True))
    keyval = (
        jax.nn.silu(keyval_sum).astype(jnp.bfloat16).reshape(rows_here, head_count, 2 * head_size)
    )
    key_rows = keyval[:, :, :head_size]
    values = keyval[:, :, head_size:]
    tail_mask = (doc_ids == tail_doc).astype(jnp.bfloat16)
    tail_state = jnp.einsum(
        "thd,the->hde",
        key_rows * tail_mask[:, None, None],
        values,
        preferred_element_type=jnp.float32,
    )
    tail_begin = doc_ends[tail_doc] - doc_lengths[tail_doc]
    restart = (tail_begin >= shard_index * rows_here).astype(jnp.float32)

    def combine(earlier, newer):
        return (newer[0] + (1.0 - newer[1]) * earlier[0], jnp.maximum(earlier[1], newer[1]))

    incoming, _ = carried_in(
        (tail_state, restart),
        "seq",
        combine,
        (jnp.zeros_like(tail_state), jnp.zeros((), jnp.float32)),
    )
    before = doc_index(jnp.reshape(shard_index * rows_here - 1, (1,)), doc_ends)[0]
    incoming = incoming * (before == first_doc).astype(jnp.float32)
    queries = jax.nn.silu(query_sum).astype(jnp.bfloat16).reshape(rows_here, head_count, head_size)
    scores = jnp.einsum("thd,shd->hts", queries, key_rows, preferred_element_type=jnp.float32)
    causal = (
        (offsets[:, None] >= offsets[None, :]) & (doc_ids[:, None] == doc_ids[None, :])
    ).astype(jnp.float32)
    weights = (scores * causal[None]).astype(jnp.bfloat16)
    within = jnp.einsum("hts,she->the", weights, values, preferred_element_type=jnp.float32)
    carried = jnp.einsum(
        "thd,hde->the", queries, incoming.astype(jnp.bfloat16), preferred_element_type=jnp.float32
    )
    carried = carried * (doc_ids == first_doc).astype(jnp.float32)[:, None, None]
    mixed = within + carried
    sum_squares = lax.psum(jnp.sum(mixed * mixed, axis=(1, 2)), "fsdp")
    inverse_rms = lax.rsqrt(sum_squares / (head_count * lax.axis_size("fsdp") * head_size) + 1e-06)
    flat = mixed.reshape(rows_here, head_count * head_size)
    return (flat * inverse_rms[:, None] * norm_gain.astype(jnp.float32)[None, :]).astype(
        jnp.bfloat16
    )


def solution(mesh):
    return jax.shard_map(
        shards,
        mesh=mesh,
        in_specs=(P("seq", None), P("seq", "fsdp", None), P("seq", "fsdp", None), P(), P("fsdp")),
        out_specs=P("seq", "fsdp"),
        check_vma=False,
    )
```

profile of v0, /device:TPU:1, one launch (start us, length us, event | category | flops | bytes accessed | tf_op | source)
XLA Modules:
  0.0 427.5 jit_solution(9087954634818524678)
XLA Ops:
  9.6 1.2 compare_convert_fusion
  10.8 120.9 %all-gather.5.cloned.1.call-done = bf16[6144,4,256]{2,1,0:T(4,128)(2,1)} async-done(((bf16[192,4,256]{2,1,0:T(4,128)(2,1)}), bf16[6144,4,256]{2,1,0:T(4,128)(2,1)}) %all-gather.5.cloned.1.call-update) | async-done | bytes 12582928 | tf_op jit(solution)/shard_map/all_gather | solution.py:41
  131.7 9.3 %copy.33 = bf16[768,8,4,256]{3,1,2,0:T(8,128)(2,1)S(1)} copy(bf16[768,8,4,256]{3,2,1,0:T(4,128)(2,1)} %bitcast.40) | data formatting | bytes 25165824
  141.0 11.5 %multiply_convert_fusion.2 = bf16[768,1024]{1,0:T(8,128)(2,1)} fusion(bf16[768,6144]{1,0:T(8,128)(2,1)S(1)} %copy-done.2, bf16[6144,1024]{1,0:T(8,128)(2,1)S(1)} %bitcast.41), kind=kOutput, calls=%fused_computation.9 | convolution fusion | flops 9667608576 | bytes 23592960 | tf_op jit(solution)/shard_map/dot_general | solution.py:38
  152.5 2.9 reshape.105
  155.4 1.4 fusion.22
  156.9 1.9 copy.31
  158.7 1.3 fusion.13
  168.0 58.6 %all-reduce = f32[32]{0:T(128)S(1)} all-reduce(f32[32]{0:T(128)S(1)} %dynamic-update-slice), channel_id=1, replica_groups=mesh['seq'=32,'fsdp'=8] {'seq'}, use_global_device_ids=true, to_apply=%add | all-reduce | flops 32 | bytes 256
  226.9 11.6 %multiply_convert_fusion.4 = bf16[768,512]{0,1:T(8,128)(2,1)} fusion(bf16[768,6144]{1,0:T(8,128)(2,1)} %param.7, bf16[768,8,4,128]{3,2,1,0:T(4,128)(2,1)} %bitcast.47), kind=kOutput, calls=%fused_computation.17 | convolution fusion | flops 4833804288 | bytes 16515072 | tf_op jit(solution)/shard_map/dot_general | solution.py:38
  238.5 79.2 %all-gather.9.cloned.1.call-done = f32[128,128,128]{2,1,0:T(8,128)} async-done(((f32[4,128,128]{2,1,0:T(8,128)}), f32[128,128,128]{2,1,0:T(8,128)}) %all-gather.9.cloned.1.call-update) | async-done | bytes 8388624 | tf_op jit(solution)/shard_map/all_gather | solution.py:9
  317.7 78.4 %while.14 = (s32[]{:T(128)}, f32[4,128,128]{2,1,0:T(8,128)S(1)}, s32[]{:T(128)}, f32[32,4,128,128]{3,2,1,0:T(8,128)}, f32[32]{0:T(128)S(1)}, /*index=5*/s32[]{:T(128)}, f32[1]{0:T(128)}, s32[]{:T(128)}) while((s32[]{:T(128)}, f32[4,128,128]{2,1,0:T(8,128)S(1)}, s32[]{:T(128)}, f32[32,4,128,128]{3,2,1,0:T(8,128)}, f32[32]{0:T(128)S(1)}, ...), condition=%wide.region_3.4_spmd.clone, body=%wide.region_2.3_spmd.clone.sunk | while | flops 262149 | bytes 786569 | solution.py:18
  319.0 1.1 fusion.34
  321.6 1.1 fusion.34
  324.1 1.1 fusion.34
  326.6 1.1 fusion.34
  329.2 1.1 fusion.34
  331.7 1.1 fusion.34
  334.2 1.1 fusion.34
  336.7 1.1 fusion.34
  396.1 2.7 fusion.19
  398.8 6.0 %fusion.10 = (f32[768]{0:T(1024)S(1)}, f32[4,128,768]{2,1,0:T(8,128)}) fusion(f32[4,128,768]{2,1,0:T(8,128)} %fusion.19, f32[768]{0:T(1024)S(1)} %get-tuple-element.130, bf16[768,4,128]{0,2,1:T(8,128)(2,1)S(1)} %copy.31, f32[768,768]{1,0:T(8,128)S(1)} %fusion.9, bf16[768,4,128]{0,2,1:T(8,128)(2,1)} %bitcast.44, bf16[768,4,128]{2,1,0:T(4,128)(2,1)} %copy-done), kind=kOutput, calls=%fused_computation.14 | convolution fusion | flops 1214250240 | bytes 7870464 | tf_op jit(solution)/shard_map/hts,she->the/dot_general | solution.py:74
  404.8 1.9 copy.25
  406.7 13.2 %psum.7 = f32[768]{0:T(1024)S(1)} all-reduce(f32[768]{0:T(1024)S(1)} %get-tuple-element.134), channel_id=1, replica_groups=mesh['seq'=32,'fsdp'=8] {'fsdp'}, use_global_device_ids=true, to_apply=%region_6.7 | all-reduce | flops 768 | bytes 6144 | tf_op jit(solution)/shard_map/psum | solution.py:80
  (86 shorter events, 54.8 us)
Async XLA Ops:
  6.5 125.1 %all-gather.5.cloned.1.call-start = ((), (), s32[]{:S(2)}) async-start(), calls=%async_computation | async-start | bytes 12976128 | tf_op jit(solution)/shard_map/all_gather | solution.py:41
  7.3 219.6 %all-gather.7.cloned.1.call-start = ((), (), s32[]{:S(2)}) async-start(), calls=%async_computation.1 | async-start | bytes 6488064 | tf_op jit(solution)/shard_map/all_gather | solution.py:40
  8.0 309.7 %all-gather.9.cloned.1.call-start = ((), (), s32[]{:S(2)}) async-start(), calls=%async_computation.2 | async-start | bytes 8650752 | tf_op jit(solution)/shard_map/all_gather | solution.py:9
  131.7 9.3 %copy-start.2 = (bf16[768,6144]{1,0:T(8,128)(2,1)S(1)}, bf16[768,6144]{1,0:T(8,128)(2,1)}, u32[]{:S(2)}) copy-start(bf16[768,6144]{1,0:T(8,128)(2,1)} %param.7) | copy-start | bytes 28311556
  156.9 11.1 %copy-start = (bf16[768,4,128]{2,1,0:T(4,128)(2,1)}, bf16[768,4,128]{2,1,0:T(4,128)(2,1)S(1)}, u32[]{:S(2)}) copy-start(bf16[768,4,128]{2,1,0:T(4,128)(2,1)S(1)} %get-tuple-element.128) | copy-start | bytes 2359300
  156.9 5.6 %copy-start.3 = (s32[8]{0:T(128)S(1)}, s32[8]{0:T(128)}, u32[]{:S(2)}) copy-start(s32[8]{0:T(128)} %param.10) | copy-start | bytes 100
  156.9 9.6 %copy-start.1 = (bf16[512]{0:T(512)(128)(2,1)S(1)}, bf16[512]{0:T(512)(128)(2,1)}, u32[]{:S(2)}) copy-start(bf16[512]{0:T(512)(128)(2,1)} %param.11) | copy-start | bytes 3076
  156.9 9.6 %copy-start.4 = (u32[256]{0:T(256)S(1)}, u32[256]{0:T(256)}, u32[]{:S(2)}) copy-start(u32[256]{0:T(256)} %constant.65) | copy-start | bytes 3076
Sparse Core Ops, SparseCore 0:
  9.9 121.7 all-gather.4
  134.3 85.5 all-gather.6
  222.5 95.1 all-gather.8
where the time goes:
time: 429 us; the launch traced here: 427 us
  waiting for transfers between devices  201 us (47%)
  blocking collectives  71.8 us (17%)
  local copies, waits for them, and re-layouts  41.2 us (10%)
  other arithmetic  39.8 us (9%)
  matrix products  33.1 us (8%)
  loops' own time  22.3 us (5%)
  between operations  17.7 us (4%)
    all_gather x1, waiting for transfers between devices, shards(): keyval_sum = project(lax.all_gather(w_keyval, 'seq', axis=0, tiled=True))  121 us
    all_gather x1, waiting for transfers between devices, carried_in(): pieces = jax.tree.map(lambda part: lax.all_gather(part, axis), value)  79.2 us
    unnamed x1, blocking collectives  58.6 us
    select_n x31, other arithmetic, step(): jnp.where(position < mine, new, old)  35.6 us
    dot_general x2, matrix products, project(): return jnp.dot(tokens, panel, preferred_element_type=jnp.float32)  23.1 us
    another operation x1, loops' own time, carried_in(): return lax.fori_loop(0, count - 1, step, running)  22.3 us
    dynamic_slice x31, local copies, waits for them, and re-layouts, step(): longer = join(running, jax.tree.map(lambda part: part[position], pieces))  20.6 us
    psum x1, blocking collectives, shards(): sum_squares = lax.psum(jnp.sum(mixed * mixed, axis=(1, 2)), 'fsdp')  13.2 us
  transfers between devices with their start and end apart: 3, of which 2 were waited for; matrix products, arithmetic and copies ran while one was open for 11% of the time, Pallas kernels for 0%

commit v1 on v0

--- a/solution.py
+++ b/solution.py
@@ -38,7 +38,11 @@
         return jnp.dot(tokens, panel, preferred_element_type=jnp.float32)
 
     query_sum = project(lax.all_gather(w_query, "seq", axis=0, tiled=True))
-    keyval_sum = project(lax.all_gather(w_keyval, "seq", axis=0, tiled=True))
+    keyval_sum = project(
+        jnp.concatenate(
+            lax.all_to_all(jnp.stack([w_keyval] * lax.axis_size("seq")), "seq", 0, 0), axis=0
+        )
+    )
     keyval = (
         jax.nn.silu(keyval_sum).astype(jnp.bfloat16).reshape(rows_here, head_count, 2 * head_size)
     )

time: 429 us -> 587 us (1.37)
  waiting for transfers between devices: 201 us -> 331 us
  blocking collectives: 71.8 us -> 84.2 us
  starting transfers between devices: 0.08 us -> 12.2 us
    all_to_all x0 -> x1, waiting for transfers between devices: none -> 313 us  [shards(): lax.all_to_all(jnp.stack([w_keyval] * lax.axis_size('seq')), 'seq', 0, 0)]
    all_gather x1 -> x0, waiting for transfers between devices: 121 us -> none  [shards(): keyval_sum = project(lax.all_gather(w_keyval, 'seq', axis=0, tiled=True))]
    all_gather x1, waiting for transfers between devices: 79.2 us -> 17.6 us  [carried_in(): pieces = jax.tree.map(lambda part: lax.all_gather(part, axis), value)]
    unnamed x1, blocking collectives: 58.6 us -> 71 us
    all_to_all x0 -> x1, starting transfers between devices: none -> 12.1 us  [shards(): lax.all_to_all(jnp.stack([w_keyval] * lax.axis_size('seq')), 'seq', 0, 0)]
    another operation x0 -> x1, local copies, waits for them, and re-layouts: none -> 7.76 us  [shards(): jnp.stack([w_keyval] * lax.axis_size('seq'))]
    unnamed x15 -> x13, local copies, waits for them, and re-layouts: 12.6 us -> 12.2 us
  transfers between devices with their start and end apart: 3 -> 3, of which waited for: 2 -> 2; matrix products, arithmetic and copies ran while one was open for 11% -> 8% of each run, Pallas kernels for 0% -> 0%
where the time goes in v1:
time: 587 us; the launch traced here: 585 us
  waiting for transfers between devices  331 us (56%)
  blocking collectives  84.2 us (14%)
  local copies, waits for them, and re-layouts  46.4 us (8%)
  other arithmetic  39.2 us (7%)
  matrix products  35.1 us (6%)
  loops' own time  18.6 us (3%)
  between operations  18.3 us (3%)
  starting transfers between devices  12.2 us (2%)
    all_to_all x1, waiting for transfers between devices, shards(): lax.all_to_all(jnp.stack([w_keyval] * lax.axis_size('seq')), 'seq', 0, 0)  313 us
    unnamed x1, blocking collectives  71 us
    select_n x31, other arithmetic, step(): jnp.where(position < mine, new, old)  35.6 us
    dot_general x2, matrix products, project(): return jnp.dot(tokens, panel, preferred_element_type=jnp.float32)  25.1 us
    another operation x1, loops' own time, carried_in(): return lax.fori_loop(0, count - 1, step, running)  18.6 us
    dynamic_slice x31, local copies, waits for them, and re-layouts, step(): longer = join(running, jax.tree.map(lambda part: part[position], pieces))  18.3 us
    all_gather x1, waiting for transfers between devices, carried_in(): pieces = jax.tree.map(lambda part: lax.all_gather(part, axis), value)  17.6 us
    psum x1, blocking collectives, shards(): sum_squares = lax.psum(jnp.sum(mixed * mixed, axis=(1, 2)), 'fsdp')  13.2 us
  transfers between devices with their start and end apart: 3, of which 2 were waited for; matrix products, arithmetic and copies ran while one was open for 8% of the time, Pallas kernels for 0%

profile of v1, /device:TPU:1, one launch (start us, length us, event | category | flops | bytes accessed | tf_op | source)
XLA Modules:
  0.0 585.3 jit_solution(2083821556025856948)
XLA Ops:
  6.5 7.8 %stack.2 = bf16[32,192,4,256]{3,2,1,0:T(4,128)(2,1)} broadcast(bf16[192,4,256]{2,1,0:T(4,128)(2,1)} %param.9), dimensions={1,2,3} | broadcast | bytes 12976128 | tf_op jit(solution)/shard_map/stack | solution.py:43
  14.3 12.1 %all-to-all-start = ((bf16[32,192,4,256]{3,2,1,0:T(4,128)(2,1)}), bf16[32,192,4,256]{3,2,1,0:T(4,128)(2,1)}, u32[]{:S(2)}, u32[]{:S(2)}) async-start(bf16[32,192,4,256]{3,2,1,0:T(4,128)(2,1)} %stack.2), calls=%async_computation | async-start | bytes 25165824 | tf_op jit(solution)/shard_map/all_to_all | solution.py:43
  28.1 1.3 compare_convert_fusion
  29.5 313.1 %all-to-all-done = bf16[32,192,4,256]{3,2,1,0:T(4,128)(2,1)} async-done(((bf16[32,192,4,256]{3,2,1,0:T(4,128)(2,1)}), bf16[32,192,4,256]{3,2,1,0:T(4,128)(2,1)}, u32[]{:S(2)}, u32[]{:S(2)}) %all-to-all-start) | async-done | bytes 12582944 | tf_op jit(solution)/shard_map/all_to_all | solution.py:43
  342.6 8.9 %copy.33 = bf16[768,8,4,256]{3,1,2,0:T(8,128)(2,1)S(1)} copy(bf16[768,8,4,256]{3,2,1,0:T(4,128)(2,1)} %bitcast.16) | data formatting | bytes 25165824
  351.5 13.2 %multiply_convert_fusion.2 = bf16[768,1024]{1,0:T(8,128)(2,1)} fusion(bf16[768,6144]{1,0:T(8,128)(2,1)} %param.7, bf16[6144,1024]{1,0:T(8,128)(2,1)S(1)} %bitcast.41), kind=kOutput, calls=%fused_computation.9 | convolution fusion | flops 9667608576 | bytes 23592960 | tf_op jit(solution)/shard_map/dot_general | solution.py:38
  364.7 2.9 reshape.103
  367.6 1.4 fusion.22
  369.1 1.8 copy.31
  370.9 1.3 fusion.13
  380.4 71.0 %all-reduce = f32[32]{0:T(128)S(1)} all-reduce(f32[32]{0:T(128)S(1)} %dynamic-update-slice), channel_id=1, replica_groups=mesh['seq'=32,'fsdp'=8] {'seq'}, use_global_device_ids=true, to_apply=%add | all-reduce | flops 32 | bytes 256
  451.6 11.9 %multiply_convert_fusion.4 = bf16[768,512]{0,1:T(8,128)(2,1)} fusion(bf16[768,6144]{1,0:T(8,128)(2,1)} %param.7, bf16[768,8,4,128]{3,2,1,0:T(4,128)(2,1)} %bitcast.47), kind=kOutput, calls=%fused_computation.17 | convolution fusion | flops 4833804288 | bytes 16515072 | tf_op jit(solution)/shard_map/dot_general | solution.py:38
  463.5 17.6 %all-gather.6.cloned.1.call-done = f32[128,128,128]{2,1,0:T(8,128)} async-done(((f32[4,128,128]{2,1,0:T(8,128)}), f32[128,128,128]{2,1,0:T(8,128)}) %all-gather.6.cloned.1.call-update) | async-done | bytes 8388624 | tf_op jit(solution)/shard_map/all_gather | solution.py:9
  481.1 72.5 %while.14 = (s32[]{:T(128)}, f32[4,128,128]{2,1,0:T(8,128)S(1)}, s32[]{:T(128)}, f32[32,4,128,128]{3,2,1,0:T(8,128)}, f32[32]{0:T(128)S(1)}, /*index=5*/s32[]{:T(128)}, f32[1]{0:T(128)}, s32[]{:T(128)}) while((s32[]{:T(128)}, f32[4,128,128]{2,1,0:T(8,128)S(1)}, s32[]{:T(128)}, f32[32,4,128,128]{3,2,1,0:T(8,128)}, f32[32]{0:T(128)S(1)}, ...), condition=%wide.region_3.4_spmd.clone, body=%wide.region_2.3_spmd.clone.sunk | while | flops 262149 | bytes 786569 | solution.py:18
  482.3 1.1 fusion.34
  487.0 1.1 fusion.34
  489.3 1.1 fusion.34
  494.0 1.1 fusion.34
  501.0 1.1 fusion.34
  508.0 1.1 fusion.34
  553.6 2.7 fusion.19
  556.3 6.0 %fusion.10 = (f32[768]{0:T(1024)S(1)}, f32[4,128,768]{2,1,0:T(8,128)}) fusion(f32[4,128,768]{2,1,0:T(8,128)} %fusion.19, f32[768]{0:T(1024)S(1)} %get-tuple-element.130, bf16[768,4,128]{0,2,1:T(8,128)(2,1)S(1)} %copy.31, f32[768,768]{1,0:T(8,128)S(1)} %fusion.9, bf16[768,4,128]{0,2,1:T(8,128)(2,1)} %bitcast.44, bf16[768,4,128]{2,1,0:T(4,128)(2,1)} %copy-done), kind=kOutput, calls=%fused_computation.14 | convolution fusion | flops 1214250240 | bytes 7870464 | tf_op jit(solution)/shard_map/hts,she->the/dot_general | solution.py:78
  562.3 1.9 copy.25
  564.2 13.2 %psum.7 = f32[768]{0:T(1024)S(1)} all-reduce(f32[768]{0:T(1024)S(1)} %get-tuple-element.134), channel_id=1, replica_groups=mesh['seq'=32,'fsdp'=8] {'fsdp'}, use_global_device_ids=true, to_apply=%region_6.7 | all-reduce | flops 768 | bytes 6144 | tf_op jit(solution)/shard_map/psum | solution.py:84
  (84 shorter events, 53.5 us)
Async XLA Ops:
  14.3 12.9 %copy-start.2 = (s32[8]{0:T(128)S(1)}, s32[8]{0:T(128)}, u32[]{:S(2)}) copy-start(s32[8]{0:T(128)} %param.10) | copy-start | bytes 100
  14.3 328.3 %all-to-all-start = ((bf16[32,192,4,256]{3,2,1,0:T(4,128)(2,1)}), bf16[32,192,4,256]{3,2,1,0:T(4,128)(2,1)}, u32[]{:S(2)}, u32[]{:S(2)}) async-start(bf16[32,192,4,256]{3,2,1,0:T(4,128)(2,1)} %stack.2), calls=%async_computation | async-start | bytes 25165824 | tf_op jit(solution)/shard_map/all_to_all | solution.py:43
  26.4 425.2 %all-gather.4.cloned.1.call-start = ((), (), s32[]{:S(2)}) async-start(), calls=%async_computation.1 | async-start | bytes 6488064 | tf_op jit(solution)/shard_map/all_gather | solution.py:40
  27.1 454.0 %all-gather.6.cloned.1.call-start = ((), (), s32[]{:S(2)}) async-start(), calls=%async_computation.2 | async-start | bytes 8650752 | tf_op jit(solution)/shard_map/all_gather | solution.py:9
  369.1 11.3 %copy-start = (bf16[768,4,128]{2,1,0:T(4,128)(2,1)}, bf16[768,4,128]{2,1,0:T(4,128)(2,1)S(1)}, u32[]{:S(2)}) copy-start(bf16[768,4,128]{2,1,0:T(4,128)(2,1)S(1)} %get-tuple-element.128) | copy-start | bytes 2359300
  369.1 9.8 %copy-start.1 = (bf16[512]{0:T(512)(128)(2,1)S(1)}, bf16[512]{0:T(512)(128)(2,1)}, u32[]{:S(2)}) copy-start(bf16[512]{0:T(512)(128)(2,1)} %param.11) | copy-start | bytes 3076
  369.1 9.8 %copy-start.3 = (u32[256]{0:T(256)S(1)}, u32[256]{0:T(256)}, u32[]{:S(2)}) copy-start(u32[256]{0:T(256)} %constant.65) | copy-start | bytes 3076
Sparse Core Ops, SparseCore 0:
  29.8 203.0 all-gather.3
  372.3 108.7 all-gather.5
